TPU v7x, 256 devices: a whole 4x4x8 slice. The times are simulated.
256 devices in a mesh: leaf: 16 (over y, x), row: 16 (over z, core).
Axes of the slice: x: 4, y: 4, z: 8, core: 2. Of those that a mesh axis runs over, the one named last changes fastest.
Arguments:
- sigma_root: float32 [2048, 2048], P(None, 'row')
- linv_one: bfloat16 [16, 2048, 2048], P('leaf', None, 'row'), as said below
- panel_one: bfloat16 [16, 512, 2048], P('leaf', None, 'row'), may hold values from -1.25 to 1.25
- tiles_one: int32 [16, 4], replicated, may hold values from 0 to 15, as said below
- mask_one: int32 [16, 4, 16], P('leaf', None, 'row'), may hold values 0 or 1
- linv_two: bfloat16 [16, 2048, 2048], P('leaf', None, 'row'), as said below
- panel_two: bfloat16 [16, 512, 2048], P('leaf', None, 'row'), may hold values from -1.25 to 1.25
- tiles_two: int32 [16, 4], replicated, may hold values from 0 to 15, as said below
- mask_two: int32 [16, 4, 16], P('leaf', None, 'row'), may hold values 0 or 1
- parent: int32 [16], replicated, may hold values from 0 to 15
Outputs:
- sigma_one: float32 [16, 2048, 2048], P('leaf', None, 'row')
- cross_one: float32 [16, 512, 2048], P('leaf', None, 'row')
- sigma_two: float32 [16, 2048, 2048], P('leaf', None, 'row')
- cross_two: float32 [16, 512, 2048], P('leaf', None, 'row')
Inputs may be any that keep to these rules, and one draw needn't show every extreme that they name: `tiles_one`: each row holds 4 different tile numbers in increasing order. `tiles_two`: each row holds 4 different tile numbers in increasing order. `linv_one`: each block is lower triangular with a positive diagonal. `sigma_root`: symmetric. `linv_two`: each block is lower triangular with a positive diagonal.
All inputs are finite; a program needn't handle non-finite values. No bound on the sum of `mask_one` or of `mask_two` on one device may be relied on, other than what follows from the above.
Results may differ from a plain program's by a relative error of at most 0.00045.
Values may be sent and summed in bfloat16 or wider, within the bound.
No kernel may reach another device: no remote copies, remote signals or barrier semaphores. Data moves between devices by JAX's collectives and lax.ppermute only.
A program may use at most 64 MiB of HBM per device.

v0:
```python
import jax
import jax.numpy as jnp
from jax import lax
from jax.sharding import PartitionSpec as P

TILE = 128


def pattern_rows(tile_list):
    offsets = jnp.arange(TILE, dtype=jnp.int32)
    return (tile_list[..., None] * TILE + offsets).reshape(tile_list.shape[:-1] + (-1,))


def expand_mask(tile_mask):
    return jnp.repeat(jnp.repeat(tile_mask, TILE, axis=0), TILE, axis=1)


def assemble(selected, row_list):
    gathered = lax.all_gather(selected, "row", axis=1, tiled=True)
    return jnp.take(gathered, row_list, axis=1)


def solve_block(selected, row_list, linv_local, panel_local, mask_local):
    select = assemble(selected, row_list)
    masked = panel_local * expand_mask(mask_local).astype(jnp.bfloat16)
    linv_wide = linv_local.astype(jnp.float32)
    whole_panel = lax.all_gather(masked, "row", axis=1, tiled=True)
    upper_part = jnp.dot(whole_panel, linv_local, preferred_element_type=jnp.float32)
    cross = -jnp.dot(select, upper_part, precision=lax.Precision.HIGHEST)
    middle = linv_wide - jnp.dot(
        whole_panel.astype(jnp.float32).T, cross, precision=lax.Precision.HIGHEST
    )
    sigma = jnp.dot(
        lax.all_gather(linv_local, "row", axis=1, tiled=True).astype(jnp.float32).T,
        middle,
        precision=lax.Precision.HIGHEST,
    )
    return (sigma, cross)


def body(
    sigma_root,
    linv_one,
    panel_one,
    tiles_one,
    mask_one,
    linv_two,
    panel_two,
    tiles_two,
    mask_two,
    parent,
):
    leaf_id = lax.axis_index("leaf")
    width = sigma_root.shape[1]
    own_tiles = lax.dynamic_index_in_dim(tiles_one, leaf_id, 0, keepdims=False)
    rows_first = pattern_rows(own_tiles)
    selected_first = jnp.take(sigma_root, rows_first, axis=0)
    sigma_first, cross_first = solve_block(
        selected_first, rows_first, linv_one[0], panel_one[0], mask_one[0]
    )
    rows_every = pattern_rows(tiles_two)
    count = rows_every.shape[0]
    block_rows = rows_every.shape[1]
    owned = (parent == leaf_id).astype(jnp.float32)
    slots = jnp.take(sigma_first, rows_every.reshape(-1), axis=0).reshape(count, block_rows, width)
    slots = slots * owned[:, None, None]
    arrived = lax.all_to_all(slots, "leaf", split_axis=0, concat_axis=0, tiled=True)
    selected_second = jnp.sum(arrived, axis=0)
    rows_second = lax.dynamic_index_in_dim(rows_every, leaf_id, 0, keepdims=False)
    sigma_second, cross_second = solve_block(
        selected_second, rows_second, linv_two[0], panel_two[0], mask_two[0]
    )
    return (sigma_first[None], cross_first[None], sigma_second[None], cross_second[None])


def solution(mesh):
    return jax.shard_map(
        body,
        mesh=mesh,
        in_specs=(
            P(None, "row"),
            P("leaf", None, "row"),
            P("leaf", None, "row"),
            P(),
            P("leaf", None, "row"),
            P("leaf", None, "row"),
            P("leaf", None, "row"),
            P(),
            P("leaf", None, "row"),
            P(),
        ),
        out_specs=(
            P("leaf", None, "row"),
            P("leaf", None, "row"),
            P("leaf", None, "row"),
            P("leaf", None, "row"),
        ),
        check_vma=False,
    )
```

profile of v0, /device:TPU:1, one launch (start us, length us, event | category | flops | bytes accessed | tf_op | source)
XLA Modules:
  0.0 404.3 jit_solution(16791441184361963141)
XLA Ops:
  7.2 0.8 convert_bitcast_fusion.1
  8.0 0.1 broadcast_bitcast_fusion.1
  8.1 1.7 bitcast_multiply_fusion.1
  9.9 0.9 multiply_reduce_fusion
  10.7 0.1 iota_add_fusion.1
  10.8 1.0 gather_fusion
  11.9 0.1 compare_and_fusion.2
  11.9 0.8 broadcast_select_fusion
  12.8 0.0 all-gather.17.cloned.1.call-start
  12.9 0.7 all-gather.17.cloned.1.call-update
  13.5 0.7 broadcast_multiply_fusion
  14.2 0.1 copy.20
  14.3 0.1 compare_select_fusion.4
  14.4 0.7 compare_convert_fusion
  15.1 0.7 convert_bitcast_fusion
  15.7 0.1 broadcast_bitcast_fusion
  15.8 0.1 iota_add_fusion
  15.9 0.1 add.146
  16.1 39.5 %all-gather.9.cloned.1.call-done = bf16[512,2048]{1,0:T(8,128)(2,1)} async-done(((bf16[512,128]{1,0:T(8,128)(2,1)}), bf16[512,2048]{1,0:T(8,128)(2,1)}) %all-gather.9.cloned.1.call-update) | async-done | bytes 2097168 | tf_op jit(solution)/shard_map/all_gather | solution.py:27
  55.5 2.3 fusion.13
  57.8 48.6 %all-gather.11.cloned.1.call-done = f32[512,2048]{1,0:T(8,128)} async-done(((f32[512,128]{1,0:T(8,128)}), f32[512,2048]{1,0:T(8,128)}) %all-gather.11.cloned.1.call-update) | async-done | bytes 4194320 | tf_op jit(solution)/shard_map/all_gather | solution.py:19
  106.5 5.3 %copy.19 = f32[512,2048]{0,1:T(8,128)} copy(f32[512,2048]{1,0:T(8,128)} %all-gather.11.cloned.1.call-done) | data formatting | bytes 8388608 | tf_op jit(solution)/shard_map/all_gather | solution.py:19
  111.8 4.2 %gather_fusion.2 = f32[512,512]{1,0:T(8,128)S(1)} fusion(f32[512,2048]{0,1:T(8,128)} %copy.19, s32[1024]{0:T(1024)S(1)} %pad_clamp_fusion.1), kind=kCustom, calls=%fused_computation.clone | custom fusion | bytes 2099200 | tf_op jit(solution)/shard_map/jit(_take)/gather | solution.py:20
  116.0 1.9 convolution_negate_fusion.1
  117.9 0.7 copy-done.4
  118.6 3.9 convolution_subtract_fusion.1
  122.6 50.3 %all-gather.17.cloned.1.call-done = bf16[1,2048,2048]{2,1,0:T(8,128)(2,1)} async-done(((bf16[1,2048,128]{2,1,0:T(8,128)(2,1)}), bf16[1,2048,2048]{2,1,0:T(8,128)(2,1)}) %all-gather.17.cloned.1.call-update) | async-done | bytes 8388624 | tf_op jit(solution)/shard_map/all_gather | solution.py:34
  172.9 6.3 %fusion.2 = f32[128,2048]{1,0:T(8,128)S(1)} fusion(f32[2048,128]{1,0:T(8,128)S(1)} %convolution_subtract_fusion.1, bf16[1,2048,2048]{2,1,0:T(8,128)(2,1)} %all-gather.17.cloned.1.call-done), kind=kOutput, calls=%fused_computation.6 | convolution fusion | flops 6442450944 | bytes 10485760 | tf_op jit(solution)/shard_map/dot_general | solution.py:33
  179.1 0.3 copy.21
  179.5 27.8 %gather_fusion.1 = f32[8192,128]{1,0:T(8,128)} fusion(f32[2048,128]{1,0:T(8,128)S(1)} %copy.21, s32[8192]{0:T(1024)S(1)} %broadcast_clamp_fusion), kind=kCustom, calls=%fused_computation.3 | custom fusion | bytes 8421376 | tf_op jit(solution)/shard_map/jit(_take)/gather | solution.py:65
  207.3 5.3 %select_multiply_fusion = f32[16,512,128]{2,1,0:T(8,128)} fusion(f32[16,512,128]{2,1,0:T(8,128)} %bitcast.84, f32[16]{0:T(128)S(1)} %compare_convert_fusion, pred[16,512]{1,0:T(8,128)(4,1)S(1)} %compare_and_fusion), kind=kLoop, calls=%fused_computation.8 | loop fusion | flops 2097152 | bytes 8396864 | tf_op jit(solution)/shard_map/mul | solution.py:66
  212.5 4.7 %all-to-all-start = ((f32[16,512,128]{2,1,0:T(8,128)}), f32[16,512,128]{2,1,0:T(8,128)}, u32[]{:S(2)}, u32[]{:S(2)}) async-start(f32[16,512,128]{2,1,0:T(8,128)} %select_multiply_fusion), calls=%async_computation | async-start | bytes 8388608 | tf_op jit(solution)/shard_map/all_to_all | solution.py:67
  217.3 0.8 bitcast_multiply_fusion
  218.1 0.0 all-gather.15.cloned.1.call-start
  218.2 62.3 %all-to-all-done = f32[16,512,128]{2,1,0:T(8,128)} async-done(((f32[16,512,128]{2,1,0:T(8,128)}), f32[16,512,128]{2,1,0:T(8,128)}, u32[]{:S(2)}, u32[]{:S(2)}) %all-to-all-start) | async-done | bytes 4194336 | tf_op jit(solution)/shard_map/all_to_all | solution.py:67
  280.5 2.4 reduce_sum.9
  282.9 0.8 copy.22
  283.7 0.2 all-gather.19.cloned.1.call-start
  284.0 0.3 all-gather.19.cloned.1.call-update
  284.4 2.3 fusion.11
  286.7 1.3 copy.23
  288.0 35.5 %all-gather.15.cloned.1.call-done = f32[512,2048]{0,1:T(8,128)} async-done(((f32[512,128]{0,1:T(8,128)}), f32[512,2048]{0,1:T(8,128)}) %all-gather.15.cloned.1.call-update) | async-done | bytes 4194320 | tf_op jit(solution)/shard_map/all_gather | solution.py:19
  323.6 4.2 %gather_fusion.3 = f32[512,512]{1,0:T(8,128)S(1)} fusion(f32[512,2048]{0,1:T(8,128)} %all-gather.15.cloned.1.call-done, s32[1024]{0:T(1024)S(1)} %pad_clamp_fusion), kind=kCustom, calls=%fused_computation.1.clone | custom fusion | bytes 2099200 | tf_op jit(solution)/shard_map/jit(_take)/gather | solution.py:20
  327.8 1.9 convolution_negate_fusion
  329.7 4.0 convolution_subtract_fusion
  333.7 56.2 %all-gather.19.cloned.1.call-done = bf16[1,2048,2048]{2,1,0:T(8,128)(2,1)} async-done(((bf16[1,2048,128]{2,1,0:T(8,128)(2,1)}), bf16[1,2048,2048]{2,1,0:T(8,128)(2,1)}) %all-gather.19.cloned.1.call-update) | async-done | bytes 8388624 | tf_op jit(solution)/shard_map/all_gather | solution.py:34
  389.9 6.3 %fusion.4 = f32[1,2048,128]{1,2,0:T(8,128)S(1)} fusion(f32[2048,128]{1,0:T(8,128)S(1)} %convolution_subtract_fusion, bf16[1,2048,2048]{2,1,0:T(8,128)(2,1)} %all-gather.19.cloned.1.call-done), kind=kOutput, calls=%fused_computation.9 | convolution fusion | flops 6442450944 | bytes 10485760 | tf_op jit(solution)/shard_map/dot_general | solution.py:33
  396.2 1.3 copy.24
  (34 shorter events, 0.4 us)
Async XLA Ops:
  7.2 3.6 copy-start
  7.2 48.4 %copy-start.1 = (bf16[1,2048,128]{2,1,0:T(8,128)(2,1)S(1)}, bf16[1,2048,128]{2,1,0:T(8,128)(2,1)}, u32[]{:S(2)}) copy-start(bf16[1,2048,128]{2,1,0:T(8,128)(2,1)} %param.13) | copy-start | bytes 1572868
  7.2 48.3 %all-gather.9.cloned.1.call-start = ((), (), s32[]{:S(2)}) async-start(), calls=%async_computation.1 | async-start | bytes 2228224 | tf_op jit(solution)/shard_map/all_gather | solution.py:27
  9.8 96.7 %all-gather.11.cloned.1.call-start = ((), (), s32[]{:S(2)}) async-start(), calls=%async_computation.2 | async-start | bytes 4456448 | tf_op jit(solution)/shard_map/all_gather | solution.py:19
  12.8 160.1 %all-gather.17.cloned.1.call-start = ((), (), s32[]{:S(2)}) async-start(), calls=%async_computation.5 | async-start | bytes 8912896 | tf_op jit(solution)/shard_map/all_gather | solution.py:34
  117.9 0.7 copy-start.4
  212.5 4.8 %copy-start.6 = (bf16[1,512,128]{2,1,0:T(8,128)(2,1)S(1)}, bf16[1,512,128]{2,1,0:T(8,128)(2,1)}, u32[]{:S(2)}) copy-start(bf16[1,512,128]{2,1,0:T(8,128)(2,1)} %param.18) | copy-start | bytes 393220
  212.5 67.9 %all-to-all-start = ((f32[16,512,128]{2,1,0:T(8,128)}), f32[16,512,128]{2,1,0:T(8,128)}, u32[]{:S(2)}, u32[]{:S(2)}) async-start(f32[16,512,128]{2,1,0:T(8,128)} %select_multiply_fusion), calls=%async_computation | async-start | bytes 8388608 | tf_op jit(solution)/shard_map/all_to_all | solution.py:67
  217.2 67.2 %copy-start.2 = (bf16[1,2048,128]{2,1,0:T(8,128)(2,1)S(1)}, bf16[1,2048,128]{2,1,0:T(8,128)(2,1)}, u32[]{:S(2)}) copy-start(bf16[1,2048,128]{2,1,0:T(8,128)(2,1)} %param.17) | copy-start | bytes 1572868
  217.2 67.2 %all-gather.13.cloned.1.call-start = ((), (), s32[]{:S(2)}) async-start(), calls=%async_computation.3 | async-start | bytes 2228224 | tf_op jit(solution)/shard_map/all_gather | solution.py:27
  218.1 105.4 %all-gather.15.cloned.1.call-start = ((), (), s32[]{:S(2)}) async-start(), calls=%async_computation.4 | async-start | bytes 4456448 | tf_op jit(solution)/shard_map/all_gather | solution.py:19
  283.7 106.2 %all-gather.19.cloned.1.call-start = ((), (), s32[]{:S(2)}) async-start(), calls=%async_computation.6 | async-start | bytes 8912896 | tf_op jit(solution)/shard_map/all_gather | solution.py:34
  288.0 41.6 %copy-start.3 = (bf16[1,2048,128]{2,1,0:T(8,128)(2,1)S(1)}, bf16[1,2048,128]{2,1,0:T(8,128)(2,1)}, u32[]{:S(2)}) copy-start(bf16[1,2048,128]{2,1,0:T(8,128)(2,1)} %param.17) | copy-start | bytes 1572868
  329.7 4.0 copy-start.5
Sparse Core Ops, SparseCore 0:
  10.4 45.1 all-gather.8
  57.9 48.5 all-gather.10
  108.2 64.6 all-gather.16
  220.1 40.0 all-gather.12
  283.9 39.6 all-gather.14
  325.2 64.6 all-gather.18
where the time goes:
time: 405 us; the launch traced here: 404 us
  waiting for transfers between devices  294 us (73%)
  local copies, waits for them, and re-layouts  47.4 us (12%)
  matrix products  28.8 us (7%)
  other arithmetic  15.1 us (4%)
  between operations  14.4 us (4%)
  starting transfers between devices  5.12 us (1%)
    all_gather x2, waiting for transfers between devices, solve_block(): lax.all_gather(linv_local, 'row', axis=1, tiled=True).astype(jnp.float32)  107 us
    all_gather x2, waiting for transfers between devices, assemble(): gathered = lax.all_gather(selected, 'row', axis=1, tiled=True)  84.1 us
    all_to_all x1, waiting for transfers between devices, body(): lax.all_to_all(slots, 'leaf', split_axis=0, concat_axis=0, tiled=True)  62.3 us
    all_gather x2, waiting for transfers between devices, solve_block(): whole_panel = lax.all_gather(masked, 'row', axis=1, tiled=True)  39.5 us
    gather x1, local copies, waits for them, and re-layouts, body(): jnp.take(sigma_first, rows_every.reshape(-1), axis=0)  27.8 us
    dot_general x2, matrix products, solve_block(): jnp.dot(lax.all_gather(linv_local, 'row', axis=1, tiled=True).astype(jnp....  12.5 us
    gather x2, local copies, waits for them, and re-layouts, assemble(): return jnp.take(gathered, row_list, axis=1)  8.43 us
  transfers between devices with their start and end apart: 7, of which 6 were waited for; matrix products, arithmetic and copies ran while one was open for 10% of the time, Pallas kernels for 0%

commit v1 on v0

--- a/solution.py
+++ b/solution.py
@@ -31,7 +31,11 @@
         whole_panel.astype(jnp.float32).T, cross, precision=lax.Precision.HIGHEST
     )
     sigma = jnp.dot(
-        lax.all_gather(linv_local, "row", axis=1, tiled=True).astype(jnp.float32).T,
+        jnp.concatenate(
+            lax.all_to_all(jnp.stack([linv_local] * lax.axis_size("row")), "row", 0, 0), axis=1
+        )
+        .astype(jnp.float32)
+        .T,
         middle,
         precision=lax.Precision.HIGHEST,
     )

time: 405 us -> 623 us (1.54)
  waiting for transfers between devices: 294 us -> 476 us
  starting transfers between devices: 5.12 us -> 23.4 us
  local copies, waits for them, and re-layouts: 47.4 us -> 58.7 us
  matrix products: 28.8 us -> 40 us
    all_gather x2, waiting for transfers between devices: 39.5 us -> 187 us  [solve_block(): whole_panel = lax.all_gather(masked, 'row', axis=1, tiled=True)]
    all_gather x2, waiting for transfers between devices: 84.1 us -> 225 us  [assemble(): gathered = lax.all_gather(selected, 'row', axis=1, tiled=True)]
    all_gather x2 -> x0, waiting for transfers between devices: 107 us -> none  [solve_block(): lax.all_gather(linv_local, 'row', axis=1, tiled=True).astype(jnp.float32)]
    all_to_all x0 -> x2, starting transfers between devices: none -> 16.3 us  [solve_block(): lax.all_to_all(jnp.stack([linv_local] * lax.axis_size('row')), 'row', 0, 0)]
    dot_general x2, matrix products: 12.5 us -> 22.6 us  [solve_block(): jnp.dot(jnp.concatenate(lax.all_to_all(jnp.stack([linv_local] * lax.axis_...]
    another operation x0 -> x2, local copies, waits for them, and re-layouts: none -> 8.6 us  [solve_block(): jnp.stack([linv_local] * lax.axis_size('row'))]
  transfers between devices with their start and end apart: 7 -> 7, of which waited for: 6 -> 5; matrix products, arithmetic and copies ran while one was open for 10% -> 7% of each run, Pallas kernels for 0% -> 0%
where the time goes in v1:
time: 623 us; the launch traced here: 622 us
  waiting for transfers between devices  476 us (76%)
  local copies, waits for them, and re-layouts  58.7 us (9%)
  matrix products  40 us (6%)
  starting transfers between devices  23.4 us (4%)
  between operations  14.1 us (2%)
  other arithmetic  10.7 us (2%)
    all_gather x2, waiting for transfers between devices, assemble(): gathered = lax.all_gather(selected, 'row', axis=1, tiled=True)  225 us
    all_gather x2, waiting for transfers between devices, solve_block(): whole_panel = lax.all_gather(masked, 'row', axis=1, tiled=True)  187 us
    all_to_all x1, waiting for transfers between devices, body(): lax.all_to_all(slots, 'leaf', split_axis=0, concat_axis=0, tiled=True)  62.7 us
    gather x1, local copies, waits for them, and re-layouts, body(): jnp.take(sigma_first, rows_every.reshape(-1), axis=0)  27.9 us
    dot_general x2, matrix products, solve_block(): jnp.dot(jnp.concatenate(lax.all_to_all(jnp.stack([linv_local] * lax.axis_...  22.6 us
    all_to_all x2, starting transfers between devices, solve_block(): lax.all_to_all(jnp.stack([linv_local] * lax.axis_size('row')), 'row', 0, 0)  16.3 us
  transfers between devices with their start and end apart: 7, of which 5 were waited for; matrix products, arithmetic and copies ran while one was open for 7% of the time, Pallas kernels for 0%

profile of v1, /device:TPU:1, one launch (start us, length us, event | category | flops | bytes accessed | tf_op | source)
XLA Modules:
  0.0 622.5 jit_solution(9794216454329186069)
XLA Ops:
  7.2 1.3 copy.27
  8.5 4.3 stack.6
  12.9 10.1 %all-to-all-start = ((bf16[16,2048,128]{1,2,0:T(8,128)(2,1)}), bf16[16,2048,128]{1,2,0:T(8,128)(2,1)}, u32[]{:S(2)}, u32[]{:S(2)}) async-start(bf16[16,2048,128]{1,2,0:T(8,128)(2,1)} %stack.6), calls=%async_computation | async-start | bytes 16777216 | tf_op jit(solution)/shard_map/all_to_all | solution.py:35
  23.0 0.0 all-gather.5.cloned.1.call-start
  23.1 0.1 broadcast_bitcast_fusion.1
  23.1 0.8 bitcast_multiply_fusion.1
  23.9 0.0 all-gather.5.cloned.1.call-update
  24.0 0.0 all-gather.7.cloned.1.call-start
  24.0 0.2 multiply_reduce_fusion
  24.2 0.1 iota_add_fusion.1
  24.3 1.0 gather_fusion
  25.3 0.1 compare_and_fusion.2
  25.4 0.8 broadcast_select_fusion
  26.3 0.1 copy.28
  26.4 0.1 compare_select_fusion.4
  26.5 0.1 iota_add_fusion
  26.6 0.1 add.146
  26.8 94.2 %all-gather.5.cloned.1.call-done = bf16[512,2048]{1,0:T(8,128)(2,1)} async-done(((bf16[512,128]{1,0:T(8,128)(2,1)}), bf16[512,2048]{1,0:T(8,128)(2,1)}) %all-gather.5.cloned.1.call-update) | async-done | bytes 2097168 | tf_op jit(solution)/shard_map/all_gather | solution.py:27
  121.0 2.3 fusion.10
  123.3 116.3 %all-gather.7.cloned.1.call-done = f32[512,2048]{1,0:T(8,128)} async-done(((f32[512,128]{1,0:T(8,128)}), f32[512,2048]{1,0:T(8,128)}) %all-gather.7.cloned.1.call-update) | async-done | bytes 4194320 | tf_op jit(solution)/shard_map/all_gather | solution.py:19
  239.6 5.5 copy.26
  245.0 5.1 gather_fusion.2
  250.1 3.1 convolution_negate_fusion.1
  253.2 3.3 convolution_subtract_fusion.1
  256.5 11.3 %fusion.14 = f32[128,2048]{1,0:T(8,128)S(1)} fusion(f32[2048,128]{1,0:T(8,128)} %convolution_subtract_fusion.1, bf16[2048,2048]{0,1:T(8,128)(2,1)} %bitcast.10), kind=kOutput, calls=%fused_computation.53 | convolution fusion | flops 6442450944 | bytes 10485760 | tf_op jit(solution)/shard_map/dot_general | solution.py:33
  267.8 0.3 copy.29
  268.1 27.9 %gather_fusion.1 = f32[8192,128]{1,0:T(8,128)} fusion(f32[2048,128]{1,0:T(8,128)S(1)} %copy.29, s32[8192]{0:T(1024)S(1)} %broadcast_clamp_fusion), kind=kCustom, calls=%fused_computation.3 | custom fusion | bytes 8421376 | tf_op jit(solution)/shard_map/jit(_take)/gather | solution.py:69
  296.1 5.3 select_multiply_fusion
  301.3 6.9 %all-to-all-start.1 = ((f32[16,512,128]{2,1,0:T(8,128)}), f32[16,512,128]{2,1,0:T(8,128)}, u32[]{:S(2)}, u32[]{:S(2)}) async-start(f32[16,512,128]{2,1,0:T(8,128)} %select_multiply_fusion), calls=%async_computation.1 | async-start | bytes 8388608 | tf_op jit(solution)/shard_map/all_to_all | solution.py:71
  308.3 0.2 copy.31
  308.5 62.7 %all-to-all-done.1 = f32[16,512,128]{2,1,0:T(8,128)} async-done(((f32[16,512,128]{2,1,0:T(8,128)}), f32[16,512,128]{2,1,0:T(8,128)}, u32[]{:S(2)}, u32[]{:S(2)}) %all-to-all-start.1) | async-done | bytes 4194336 | tf_op jit(solution)/shard_map/all_to_all | solution.py:71
  371.2 4.3 stack.7
  375.5 6.2 all-to-all-start.2
  381.6 0.0 all-gather.9.cloned.1.call-start
  381.7 0.1 broadcast_bitcast_fusion
  381.8 0.8 bitcast_multiply_fusion
  382.6 0.0 all-gather.11.cloned.1.call-start
  382.6 2.4 reduce_sum.9
  385.0 0.8 copy.30
  386.0 93.2 %all-gather.9.cloned.1.call-done = bf16[512,2048]{1,0:T(8,128)(2,1)} async-done(((bf16[512,128]{1,0:T(8,128)(2,1)}), bf16[512,2048]{1,0:T(8,128)(2,1)}) %all-gather.9.cloned.1.call-update) | async-done | bytes 2097168 | tf_op jit(solution)/shard_map/all_gather | solution.py:27
  479.2 2.3 fusion.8
  481.5 1.3 copy.32
  482.8 109.2 %all-gather.11.cloned.1.call-done = f32[512,2048]{0,1:T(8,128)} async-done(((f32[512,128]{0,1:T(8,128)}), f32[512,2048]{0,1:T(8,128)}) %all-gather.11.cloned.1.call-update) | async-done | bytes 4194320 | tf_op jit(solution)/shard_map/all_gather | solution.py:19
  591.9 4.9 gather_fusion.3
  596.8 3.1 convolution_negate_fusion
  600.0 3.3 convolution_subtract_fusion
  603.3 11.4 %convolution_bitcast_fusion = f32[1,2048,128]{1,2,0:T(8,128)S(1)} fusion(f32[2048,128]{1,0:T(8,128)} %convolution_subtract_fusion, bf16[2048,2048]{0,1:T(8,128)(2,1)} %bitcast.24), kind=kOutput, calls=%fused_computation.5 | convolution fusion | flops 6442450944 | bytes 10485760 | tf_op jit(solution)/shard_map/dot_general | solution.py:33
  614.6 1.3 copy.33
  (54 shorter events, 0.3 us)
Async XLA Ops:
  7.2 17.1 %copy-start = (f32[2048,128]{1,0:T(8,128)S(1)}, f32[2048,128]{1,0:T(8,128)}, u32[]{:S(2)}) copy-start(f32[2048,128]{1,0:T(8,128)} %param.12) | copy-start | bytes 3145732
  12.8 10.2 %copy-start.13 = (s32[1,4,1]{1,2,0:T(1,128)S(1)}, s32[1,4,1]{1,2,0:T(1,128)}, u32[]{:S(2)}) copy-start(s32[1,4,1]{1,2,0:T(1,128)} %param.16) | copy-start | bytes 52
  12.8 10.3 %copy-start.9 = (bf16[1,512,128]{2,1,0:T(8,128)(2,1)S(1)}, bf16[1,512,128]{2,1,0:T(8,128)(2,1)}, u32[]{:S(2)}) copy-start(bf16[1,512,128]{2,1,0:T(8,128)(2,1)} %param.14) | copy-start | bytes 393220
  12.8 11.2 %copy-start.11 = (s32[16,4]{0,1:T(4,128)S(1)}, s32[16,4]{0,1:T(4,128)}, u32[]{:S(2)}) copy-start(s32[16,4]{0,1:T(4,128)} %param.15) | copy-start | bytes 772
  12.8 13.5 %copy-start.12 = (s32[16,4]{0,1:T(4,128)S(1)}, s32[16,4]{0,1:T(4,128)}, u32[]{:S(2)}) copy-start(s32[16,4]{0,1:T(4,128)} %param.19) | copy-start | bytes 772
  12.8 13.6 %copy-start.14 = (s32[16]{0:T(128)S(1)}, s32[16]{0:T(128)}, u32[]{:S(2)}) copy-start(s32[16]{0:T(128)} %param.21) | copy-start | bytes 196
  12.9 108.1 %copy-start.4 = (bf16[1,2048,128]{2,1,0:T(8,128)(2,1)S(1)}, bf16[1,2048,128]{2,1,0:T(8,128)(2,1)}, u32[]{:S(2)}) copy-start(bf16[1,2048,128]{2,1,0:T(8,128)(2,1)} %param.13) | copy-start | bytes 1572868
  12.9 243.6 %all-to-all-start = ((bf16[16,2048,128]{1,2,0:T(8,128)(2,1)}), bf16[16,2048,128]{1,2,0:T(8,128)(2,1)}, u32[]{:S(2)}, u32[]{:S(2)}) async-start(bf16[16,2048,128]{1,2,0:T(8,128)(2,1)} %stack.6), calls=%async_computation | async-start | bytes 16777216 | tf_op jit(solution)/shard_map/all_to_all | solution.py:35
  23.0 98.0 %all-gather.5.cloned.1.call-start = ((), (), s32[]{:S(2)}) async-start(), calls=%async_computation.3 | async-start | bytes 2228224 | tf_op jit(solution)/shard_map/all_gather | solution.py:27
  24.0 215.6 %all-gather.7.cloned.1.call-start = ((), (), s32[]{:S(2)}) async-start(), calls=%async_computation.4 | async-start | bytes 4456448 | tf_op jit(solution)/shard_map/all_gather | solution.py:19
  245.0 8.2 %copy-start.2 = (bf16[512,2048]{1,0:T(8,128)(2,1)S(1)}, bf16[512,2048]{1,0:T(8,128)(2,1)}, u32[]{:S(2)}) copy-start(bf16[512,2048]{1,0:T(8,128)(2,1)} %all-gather.5.cloned.1.call-done) | copy-start | bytes 6291460
  245.0 8.2 %copy-start.5 = (bf16[1,2048,128]{2,1,0:T(8,128)(2,1)S(1)}, bf16[1,2048,128]{2,1,0:T(8,128)(2,1)}, u32[]{:S(2)}) copy-start(bf16[1,2048,128]{2,1,0:T(8,128)(2,1)} %param.13) | copy-start | bytes 1572868
  253.2 14.6 %copy-start.7 = (f32[512,128]{1,0:T(8,128)}, f32[512,128]{1,0:T(8,128)S(1)}, u32[]{:S(2)}) copy-start(f32[512,128]{1,0:T(8,128)S(1)} %convolution_negate_fusion.1) | copy-start | bytes 786436
  301.3 7.0 %copy-start.6 = (bf16[1,2048,128]{2,1,0:T(8,128)(2,1)S(1)}, bf16[1,2048,128]{2,1,0:T(8,128)(2,1)}, u32[]{:S(2)}) copy-start(bf16[1,2048,128]{2,1,0:T(8,128)(2,1)} %param.17) | copy-start | bytes 1572868
  301.3 69.9 %all-to-all-start.1 = ((f32[16,512,128]{2,1,0:T(8,128)}), f32[16,512,128]{2,1,0:T(8,128)}, u32[]{:S(2)}, u32[]{:S(2)}) async-start(f32[16,512,128]{2,1,0:T(8,128)} %select_multiply_fusion), calls=%async_computation.1 | async-start | bytes 8388608 | tf_op jit(solution)/shard_map/all_to_all | solution.py:71
  375.5 6.2 copy-start.15
  375.5 6.3 %copy-start.10 = (bf16[1,512,128]{2,1,0:T(8,128)(2,1)S(1)}, bf16[1,512,128]{2,1,0:T(8,128)(2,1)}, u32[]{:S(2)}) copy-start(bf16[1,512,128]{2,1,0:T(8,128)(2,1)} %param.18) | copy-start | bytes 393220
  375.5 227.8 %all-to-all-start.2 = ((bf16[16,2048,128]{1,2,0:T(8,128)(2,1)}), bf16[16,2048,128]{1,2,0:T(8,128)(2,1)}, u32[]{:S(2)}, u32[]{:S(2)}) async-start(bf16[16,2048,128]{1,2,0:T(8,128)(2,1)} %stack.7), calls=%async_computation.2 | async-start | bytes 16777216 | tf_op jit(solution)/shard_map/all_to_all | solution.py:35
  381.6 97.5 %all-gather.9.cloned.1.call-start = ((), (), s32[]{:S(2)}) async-start(), calls=%async_computation.5 | async-start | bytes 2228224 | tf_op jit(solution)/shard_map/all_gather | solution.py:27
  382.6 209.4 %all-gather.11.cloned.1.call-start = ((), (), s32[]{:S(2)}) async-start(), calls=%async_computation.6 | async-start | bytes 4456448 | tf_op jit(solution)/shard_map/all_gather | solution.py:19
  482.8 117.2 %copy-start.3 = (bf16[512,2048]{1,0:T(8,128)(2,1)S(1)}, bf16[512,2048]{1,0:T(8,128)(2,1)}, u32[]{:S(2)}) copy-start(bf16[512,2048]{1,0:T(8,128)(2,1)} %all-gather.9.cloned.1.call-done) | copy-start | bytes 6291460
  600.0 14.7 %copy-start.8 = (f32[512,128]{1,0:T(8,128)}, f32[512,128]{1,0:T(8,128)S(1)}, u32[]{:S(2)}) copy-start(f32[512,128]{1,0:T(8,128)S(1)} %convolution_negate_fusion) | copy-start | bytes 786436
  603.3 12.7 %copy-start.1 = (f32[2048,128]{1,0:T(8,128)S(1)}, f32[2048,128]{1,0:T(8,128)}, u32[]{:S(2)}) copy-start(f32[2048,128]{1,0:T(8,128)} %param.12) | copy-start | bytes 3145732
Sparse Core Ops, SparseCore 0:
  26.2 94.7 all-gather.4
  123.3 116.2 all-gather.6
  384.8 94.3 all-gather.8
  481.4 110.4 all-gather.10
